TPU v7x, 32 devices: a whole 2x2x4 slice. The times are simulated.
32 devices in a mesh: ctx: 16 (over z, y, core), head: 2 (over x).
Axes of the slice: x: 2, y: 2, z: 4, core: 2. Of those that a mesh axis runs over, the one named last changes fastest.
Arguments:
- queries: bfloat16 [12288, 1024], P(('ctx', 'head')), may hold values from -64 to 64
- keys: bfloat16 [12288, 256], P(('ctx', 'head')), may hold values from -6 to 6
- values: bfloat16 [12288, 256], P(('ctx', 'head')), may hold values from -6 to 6
- out_grad: bfloat16 [12288, 1024], P(('ctx', 'head')), may hold values from -6 to 6
- rand_blocks: int32 [96, 3], replicated, may hold values from 0 to 95, as said below
- rand_count: int32 [96], replicated, may hold values from 1 to 3
Outputs:
- query_grad: bfloat16 [12288, 1024], P('ctx', 'head')
- key_grad: bfloat16 [12288, 256], P('ctx', 'head')
- value_grad: bfloat16 [12288, 256], P('ctx', 'head')
Inputs may be any that keep to these rules, and one draw needn't show every extreme that they name: Entry rand_blocks[b, r] names a block of a ctx shard (a range of 6 blocks) that is neither b's own shard nor either neighbour of it, counted modulo 16. The 18 entries of one shard's query blocks name blocks of one other shard at most 2 times, exactly 2 times for some shard.
All inputs are finite; a program needn't handle non-finite values.
Results may differ from a plain program's by a relative error of at most 0.0087.
Values may be sent and summed in bfloat16 or wider, within the bound.
A program may use at most 64 MiB of HBM per device.

v0:
```python
import math
import jax
import jax.numpy as jnp
from jax import lax
from jax.sharding import PartitionSpec as P

BLOCK = 128
HD = 128
GROUP = 4
G = 2
RAND = 3
QB_DEV = 6
NKB = 8


def broadcast(array, axis, root):
    mine = lax.axis_index(axis) == root
    return lax.psum(jnp.where(mine, array, jnp.zeros_like(array)), axis)


def attend(unused, inputs):
    query_tile, grad_tile, pair_tile, mask_row = inputs
    factor = 1.0 / math.sqrt(HD)
    key_tile = pair_tile[:, :, :HD].reshape(NKB * BLOCK, HD)
    value_tile = pair_tile[:, :, HD:].reshape(NKB * BLOCK, HD)
    key_mask = jnp.repeat(mask_row, BLOCK)
    scores = (
        jnp.einsum("tgh,kh->tgk", query_tile, key_tile, preferred_element_type=jnp.float32) * factor
    )
    scores = jnp.where(key_mask[None, None, :], scores, -jnp.inf)
    row_max = jnp.max(scores, axis=-1, keepdims=True)
    raw_weights = jnp.exp(scores - row_max)
    weights = raw_weights / jnp.sum(raw_weights, axis=-1, keepdims=True)
    weights_low = weights.astype(jnp.bfloat16)
    output = jnp.einsum("tgk,kh->tgh", weights_low, value_tile, preferred_element_type=jnp.float32)
    row_dot = jnp.sum(grad_tile.astype(jnp.float32) * output, axis=-1, keepdims=True)
    dprobs = jnp.einsum("tgh,kh->tgk", grad_tile, value_tile, preferred_element_type=jnp.float32)
    dscores = (weights * (dprobs - row_dot)).astype(jnp.bfloat16)
    dquery = (
        jnp.einsum("tgk,kh->tgh", dscores, key_tile, preferred_element_type=jnp.float32) * factor
    ).astype(jnp.bfloat16)
    key_part = (
        jnp.einsum("tgk,tgh->kh", dscores, query_tile, preferred_element_type=jnp.float32) * factor
    )
    value_part = jnp.einsum(
        "tgk,tgh->kh", weights_low, grad_tile, preferred_element_type=jnp.float32
    )
    pair_grad = jnp.concatenate(
        [key_part.reshape(NKB, BLOCK, HD), value_part.reshape(NKB, BLOCK, HD)], axis=-1
    )
    return (unused, (dquery, pair_grad))


def body(queries, keys, values, out_grad, rand_blocks, rand_count):
    head_queries, head_keys, head_values, head_grads = (
        lax.all_to_all(queries, "head", split_axis=1, concat_axis=0, tiled=True),
        lax.all_to_all(keys, "head", split_axis=1, concat_axis=0, tiled=True),
        lax.all_to_all(values, "head", split_axis=1, concat_axis=0, tiled=True),
        lax.all_to_all(out_grad, "head", split_axis=1, concat_axis=0, tiled=True),
    )
    shards = lax.axis_size("ctx")
    myself = lax.axis_index("ctx")
    per_dev = QB_DEV
    entries = per_dev * RAND
    owners_used = min(entries, shards - 3)
    capacity = (entries + owners_used - 1) // owners_used
    total_blocks = per_dev * shards
    far_slots = shards * capacity
    local_pairs = jnp.concatenate([head_keys, head_values], axis=1).reshape(per_dev, BLOCK, 2 * HD)
    global_pairs = broadcast(local_pairs[:G], "ctx", 0)
    flat_blocks = rand_blocks.reshape(shards, entries)
    owners = flat_blocks // per_dev
    offsets = flat_blocks % per_dev
    positions = jnp.arange(entries, dtype=jnp.int32)
    earlier = positions[None, :] < positions[:, None]
    same_owner = owners[:, :, None] == owners[:, None, :]
    slot_ranks = jnp.sum(same_owner & earlier[None], axis=2)
    slot_range = jnp.arange(capacity, dtype=jnp.int32)
    send_hits = (
        (owners == myself)[:, None, :] & (slot_ranks[:, None, :] == slot_range[None, :, None])
    ).astype(jnp.float32)
    offset_hot = (
        offsets[:, :, None] == jnp.arange(per_dev, dtype=jnp.int32)[None, None, :]
    ).astype(jnp.float32)
    send_table = jnp.einsum("dme,deq->dmq", send_hits, offset_hot)
    edge_base = per_dev + far_slots
    targets = jnp.arange(shards, dtype=jnp.int32)[:, None, None]
    first_slot = (slot_range == 0)[None, :, None]
    block_range = jnp.arange(per_dev, dtype=jnp.int32)[None, None, :]
    right_send = (targets == (myself + 1) % shards) & first_slot & (block_range == per_dev - 1)
    left_send = (targets == (myself - 1 + shards) % shards) & first_slot & (block_range == 0)
    send_table = send_table + right_send.astype(jnp.float32) + left_send.astype(jnp.float32)
    edge_pairs = jnp.zeros((0, BLOCK, 2 * HD), jnp.bfloat16)
    left_far = per_dev + (myself - 1 + shards) % shards * capacity
    right_far = per_dev + (myself + 1) % shards * capacity
    outgoing = jnp.einsum(
        "dmq,qtc->dmtc",
        send_table.astype(jnp.bfloat16),
        local_pairs,
        preferred_element_type=jnp.float32,
    ).astype(jnp.bfloat16)
    far_pairs = lax.all_to_all(outgoing, "ctx", split_axis=0, concat_axis=0, tiled=True)
    block_pool = jnp.concatenate(
        [local_pairs, far_pairs.reshape(far_slots, BLOCK, 2 * HD), edge_pairs, global_pairs], axis=0
    )
    local_index = jnp.arange(per_dev, dtype=jnp.int32)
    seq_block = myself * per_dev + local_index
    left_index = jnp.where(local_index > 0, local_index - 1, left_far)
    right_index = jnp.where(local_index < per_dev - 1, local_index + 1, right_far)
    global_index = jnp.broadcast_to(
        edge_base + jnp.arange(G, dtype=jnp.int32)[None, :], (per_dev, G)
    )
    my_owners = lax.dynamic_index_in_dim(owners, myself, 0, keepdims=False)
    my_ranks = lax.dynamic_index_in_dim(slot_ranks, myself, 0, keepdims=False)
    random_index = (per_dev + my_owners * capacity + my_ranks).reshape(per_dev, RAND)
    key_table = jnp.concatenate(
        [jnp.stack([left_index, local_index, right_index], axis=1), global_index, random_index],
        axis=1,
    )
    my_counts = lax.dynamic_slice_in_dim(rand_count, myself * per_dev, per_dev)
    key_valid = jnp.concatenate(
        [
            jnp.stack([seq_block > 0, seq_block >= 0, seq_block < total_blocks - 1], axis=1),
            jnp.ones((per_dev, G), bool),
            jnp.arange(RAND, dtype=jnp.int32)[None, :] < my_counts[:, None],
        ],
        axis=1,
    )
    remote = (key_table >= per_dev) & (key_table < edge_base)
    gathered = block_pool[key_table]
    query_tiles = head_queries.reshape(per_dev, BLOCK, GROUP, HD)
    grad_tiles = head_grads.reshape(per_dev, BLOCK, GROUP, HD)
    unused, (dq_tiles, pair_grads) = lax.scan(
        attend, jnp.zeros((), jnp.float32), (query_tiles, grad_tiles, gathered, key_valid)
    )
    lowered = lax.optimization_barrier(pair_grads.astype(jnp.bfloat16)).astype(jnp.float32)
    pair_grads = jnp.where(remote[:, :, None, None], lowered, pair_grads)
    pool_size = edge_base + G
    pool_hot = (
        key_table[:, :, None] == jnp.arange(pool_size, dtype=jnp.int32)[None, None, :]
    ).astype(jnp.float32)
    pool_grads = jnp.einsum("jnp,jntc->ptc", pool_hot, pair_grads, precision=lax.Precision.HIGHEST)
    local_grads = pool_grads[:per_dev]
    outgoing_grads = (
        pool_grads[per_dev:edge_base].reshape(shards, capacity, BLOCK, 2 * HD).astype(jnp.bfloat16)
    )
    returned = lax.all_to_all(outgoing_grads, "ctx", split_axis=0, concat_axis=0, tiled=True)
    local_grads = local_grads + jnp.einsum(
        "dmq,dmtc->qtc", send_table, returned.astype(jnp.float32), precision=lax.Precision.HIGHEST
    )
    global_total = lax.psum(pool_grads[edge_base:], "ctx")
    local_grads = local_grads.at[:G].add(
        jnp.where(myself == 0, global_total, jnp.zeros_like(global_total))
    )
    query_grad = dq_tiles.reshape(per_dev * BLOCK, GROUP * HD)
    key_grad = local_grads[:, :, :HD].reshape(per_dev * BLOCK, HD).astype(jnp.bfloat16)
    value_grad = local_grads[:, :, HD:].reshape(per_dev * BLOCK, HD).astype(jnp.bfloat16)
    return (query_grad, key_grad, value_grad)


def solution(mesh):
    placed = (
        P(("ctx", "head"), None),
        P(("ctx", "head"), None),
        P(("ctx", "head"), None),
        P(("ctx", "head"), None),
        P(),
        P(),
    )
    return jax.shard_map(
        body,
        mesh=mesh,
        in_specs=placed,
        out_specs=(P("ctx", "head"), P("ctx", "head"), P("ctx", "head")),
        check_vma=False,
    )
```

profile of v0, /device:TPU:0, one launch (start us, length us, event | category | flops | bytes accessed | tf_op | source)
XLA Modules:
  0.0 388.8 jit_solution(16370104756201506846)
XLA Ops:
  7.2 1.8 copy.167
  9.0 4.2 %all-to-all-start.2 = ((bf16[384,2,128]{0,2,1:T(8,128)(2,1)}), bf16[384,2,128]{0,2,1:T(8,128)(2,1)S(1)}, u32[]{:S(2)}, u32[]{:S(2)}) async-start(bf16[384,2,128]{0,2,1:T(8,128)(2,1)} %bitcast.24), calls=%async_computation.2 | async-start | bytes 393216 | tf_op jit(solution)/shard_map/all_to_all | solution.py:58
  14.6 2.1 copy.243
  19.0 3.5 all-to-all-start.1
  22.4 5.1 %all-to-all-done.1 = bf16[384,2,128]{0,2,1:T(8,128)(2,1)S(1)} async-done(((bf16[384,2,128]{0,2,1:T(8,128)(2,1)}), bf16[384,2,128]{0,2,1:T(8,128)(2,1)S(1)}, u32[]{:S(2)}, u32[]{:S(2)}) %all-to-all-start.1) | async-done | bytes 196640 | tf_op jit(solution)/shard_map/all_to_all | solution.py:57
  27.6 3.5 all-to-all-start
  32.7 8.9 %all-to-all-done = bf16[384,2,512]{2,0,1:T(8,128)(2,1)S(1)} async-done(((bf16[384,2,512]{2,0,1:T(8,128)(2,1)}), bf16[384,2,512]{2,0,1:T(8,128)(2,1)S(1)}, u32[]{:S(2)}, u32[]{:S(2)}) %all-to-all-start) | async-done | bytes 786464 | tf_op jit(solution)/shard_map/all_to_all | solution.py:56
  41.6 3.5 all-to-all-start.4
  46.2 2.1 copy.177
  48.3 6.4 %all-to-all-done.4 = bf16[384,2,512]{2,0,1:T(8,128)(2,1)S(1)} async-done(((bf16[384,2,512]{2,0,1:T(8,128)(2,1)}), bf16[384,2,512]{2,0,1:T(8,128)(2,1)S(1)}, u32[]{:S(2)}, u32[]{:S(2)}) %all-to-all-start.4) | async-done | bytes 786464 | tf_op jit(solution)/shard_map/all_to_all | solution.py:59
  55.7 5.1 %all-to-all-start.3 = ((bf16[16,2,128,256]{3,2,1,0:T(8,128)(2,1)}), bf16[16,2,128,256]{3,2,1,0:T(8,128)(2,1)S(1)}, u32[]{:S(2)}, u32[]{:S(2)}) async-start(bf16[16,2,128,256]{3,2,1,0:T(8,128)(2,1)} %copy.177), calls=%async_computation.3 | async-start | bytes 4194304 | tf_op jit(solution)/shard_map/all_to_all | solution.py:102
  62.9 1.5 fusion.29
  66.4 1.7 reshape.537
  68.1 104.0 %all-reduce.3.cloned.1.call-done = bf16[2,128,256]{2,1,0:T(8,128)(2,1)} async-done(((bf16[2,128,256]{2,1,0:T(8,128)(2,1)}), bf16[2,128,256]{2,1,0:T(8,128)(2,1)}) %all-reduce.3.cloned.1.call-update) | async-done | bytes 131088 | tf_op jit(solution)/shard_map/psum | solution.py:18
  172.1 1.4 copy-done.2
  173.5 2.0 pad_maximum_fusion
  175.5 2.6 gather_fusion
  178.1 49.3 %while.13 = (s32[]{:T(128)}, bf16[6,128,4,128]{3,2,1,0:T(4,128)(2,1)}, f32[6,8,128,256]{2,3,1,0:T(8,128)}, pred[6,8]{1,0:T(8,128)(4,1)S(1)}, bf16[6,128,4,128]{3...) while((s32[]{:T(128)}, ...), condition=%wide.region_6.7_spmd, body=%wide.region_2.6_spmd.sunk | while | flops 814414336 | bytes 22569096 | solution.py:133
  227.4 3.4 convert_element_type.57
  232.0 3.9 convert_select_fusion
  235.9 6.7 %copy.188 = f32[6,8,128,256]{3,1,0,2:T(8,128)} copy(f32[6,8,128,256]{2,3,1,0:T(8,128)} %convert_select_fusion) | data formatting | bytes 12582912 | tf_op jit(solution)/shard_map/jit(_where)/select_n | solution.py:137
  242.6 5.0 %convolution_bitcast_fusion.2 = f32[40,128,256]{2,0,1:T(8,128)S(1)} fusion(f32[6,8,128,256]{3,1,0,2:T(8,128)} %copy.188, s32[6,8]{1,0:T(8,128)S(1)} %concatenate.68), kind=kOutput, calls=%fused_computation.38 | convolution fusion | flops 754976640 | bytes 11534528 | tf_op jit(solution)/shard_map/jnp,jntc->ptc/dot_general | solution.py:142
  247.6 2.3 copy-done.1
  249.9 2.0 slice.74
  251.9 2.7 convert_element_type.59
  254.7 3.4 copy.189
  258.1 6.7 %all-to-all-start.5 = ((bf16[16,2,128,256]{3,1,2,0:T(2,128)(2,1)}), bf16[16,2,128,256]{3,1,2,0:T(2,128)(2,1)S(1)}, u32[]{:S(2)}, u32[]{:S(2)}) async-start(bf16[16,2,128,256]{3,1,2,0:T(2,128)(2,1)} %copy.189), calls=%async_computation.5 | async-start | bytes 4194304 | tf_op jit(solution)/shard_map/all_to_all | solution.py:147
  264.8 2.0 slice.66
  267.9 39.2 %all-to-all-done.5 = bf16[16,2,128,256]{3,1,2,0:T(2,128)(2,1)S(1)} async-done(((bf16[16,2,128,256]{3,1,2,0:T(2,128)(2,1)}), bf16[16,2,128,256]{3,1,2,0:T(2,128)(2,1)S(1)}, u32[]{:S(2)}, u32[]{:S(2)}) %all-to-all-start.5) | async-done | bytes 2097184 | tf_op jit(solution)/shard_map/all_to_all | solution.py:147
  307.1 3.2 fusion.24
  310.4 68.8 %all-reduce.5.cloned.1.call-done = f32[2,128,256]{2,0,1:T(2,128)} async-done(((f32[2,128,256]{2,0,1:T(2,128)}), f32[2,128,256]{2,0,1:T(2,128)}) %all-reduce.5.cloned.1.call-update) | async-done | bytes 262160 | tf_op jit(solution)/shard_map/psum | solution.py:151
  379.1 1.2 fusion.28
  (173 shorter events, 63.8 us)
Async XLA Ops:
  7.2 9.6 %copy-start.8 = (bf16[384,256]{1,0:T(8,128)(2,1)S(1)}, bf16[384,256]{1,0:T(8,128)(2,1)}, u32[]{:S(2)}) copy-start(bf16[384,256]{1,0:T(8,128)(2,1)} %param.11) | copy-start | bytes 589828
  9.0 10.0 %all-to-all-start.2 = ((bf16[384,2,128]{0,2,1:T(8,128)(2,1)}), bf16[384,2,128]{0,2,1:T(8,128)(2,1)S(1)}, u32[]{:S(2)}, u32[]{:S(2)}) async-start(bf16[384,2,128]{0,2,1:T(8,128)(2,1)} %bitcast.24), calls=%async_computation.2 | async-start | bytes 393216 | tf_op jit(solution)/shard_map/all_to_all | solution.py:58
  14.6 16.7 %copy-start.6 = (bf16[384,1024]{1,0:T(8,128)(2,1)S(1)}, bf16[384,1024]{1,0:T(8,128)(2,1)}, u32[]{:S(2)}) copy-start(bf16[384,1024]{1,0:T(8,128)(2,1)} %param.13) | copy-start | bytes 2359300
  19.0 8.6 %all-to-all-start.1 = ((bf16[384,2,128]{0,2,1:T(8,128)(2,1)}), bf16[384,2,128]{0,2,1:T(8,128)(2,1)S(1)}, u32[]{:S(2)}, u32[]{:S(2)}) async-start(bf16[384,2,128]{0,2,1:T(8,128)(2,1)} %bitcast.21), calls=%async_computation.1 | async-start | bytes 393216 | tf_op jit(solution)/shard_map/all_to_all | solution.py:57
  27.6 14.0 %all-to-all-start = ((bf16[384,2,512]{2,0,1:T(8,128)(2,1)}), bf16[384,2,512]{2,0,1:T(8,128)(2,1)S(1)}, u32[]{:S(2)}, u32[]{:S(2)}) async-start(bf16[384,2,512]{2,0,1:T(8,128)(2,1)} %bitcast.127), calls=%async_computation | async-start | bytes 1572864 | tf_op jit(solution)/shard_map/all_to_all | solution.py:56
  32.4 13.8 %copy-start.4 = (bf16[2,384,128]{2,1,0:T(8,128)(2,1)}, bf16[2,384,128]{2,1,0:T(8,128)(2,1)S(1)}, u32[]{:S(2)}) copy-start(bf16[2,384,128]{2,1,0:T(8,128)(2,1)S(1)} %copy.168) | copy-start | bytes 589828
  32.6 9.0 %copy-start.5 = (bf16[2,384,128]{2,1,0:T(8,128)(2,1)}, bf16[2,384,128]{2,1,0:T(8,128)(2,1)S(1)}, u32[]{:S(2)}) copy-start(bf16[2,384,128]{2,1,0:T(8,128)(2,1)S(1)} %copy.166) | copy-start | bytes 589828
  41.6 13.1 %all-to-all-start.4 = ((bf16[384,2,512]{2,0,1:T(8,128)(2,1)}), bf16[384,2,512]{2,0,1:T(8,128)(2,1)S(1)}, u32[]{:S(2)}, u32[]{:S(2)}) async-start(bf16[384,2,512]{2,0,1:T(8,128)(2,1)} %bitcast.126), calls=%async_computation.4 | async-start | bytes 1572864 | tf_op jit(solution)/shard_map/all_to_all | solution.py:59
  48.3 14.2 %copy-start.9 = (s32[96]{0:T(128)S(1)}, s32[96]{0:T(128)}, u32[]{:S(2)}) copy-start(s32[96]{0:T(128)} %param.15) | copy-start | bytes 1156
  54.7 1.0 copy-start.3
  55.7 116.4 %all-to-all-start.3 = ((bf16[16,2,128,256]{3,2,1,0:T(8,128)(2,1)}), bf16[16,2,128,256]{3,2,1,0:T(8,128)(2,1)S(1)}, u32[]{:S(2)}, u32[]{:S(2)}) async-start(bf16[16,2,128,256]{3,2,1,0:T(8,128)(2,1)} %copy.177), calls=%async_computation.3 | async-start | bytes 4194304 | tf_op jit(solution)/shard_map/all_to_all | solution.py:102
  60.8 111.4 %all-reduce.3.cloned.1.call-start = ((), (), s32[]{:S(2)}) async-start(), calls=%async_computation.6 | async-start | bytes 262144 | tf_op jit(solution)/shard_map/psum | solution.py:18
  172.1 1.4 copy-start.2
  227.4 4.6 %copy-start = (f32[6,8,128,256]{2,3,1,0:T(8,128)S(1)}, f32[6,8,128,256]{2,3,1,0:T(8,128)}, u32[]{:S(2)}) copy-start(f32[6,8,128,256]{2,3,1,0:T(8,128)} %get-tuple-element.54) | copy-start | bytes 18874372
  247.6 2.3 copy-start.1
  258.1 8.8 %copy-start.7 = (bf16[6,128,4,128]{3,2,1,0:T(4,128)(2,1)S(1)}, bf16[6,128,4,128]{3,2,1,0:T(4,128)(2,1)}, u32[]{:S(2)}) copy-start(bf16[6,128,4,128]{3,2,1,0:T(4,128)(2,1)} %get-tuple-element.53) | copy-start | bytes 2359300
  258.1 49.1 %all-to-all-start.5 = ((bf16[16,2,128,256]{3,1,2,0:T(2,128)(2,1)}), bf16[16,2,128,256]{3,1,2,0:T(2,128)(2,1)S(1)}, u32[]{:S(2)}, u32[]{:S(2)}) async-start(bf16[16,2,128,256]{3,1,2,0:T(2,128)(2,1)} %copy.189), calls=%async_computation.5 | async-start | bytes 4194304 | tf_op jit(solution)/shard_map/all_to_all | solution.py:147
  264.8 114.4 %all-reduce.5.cloned.1.call-start = ((), (), s32[]{:S(2)}) async-start(), calls=%async_computation.7 | async-start | bytes 524288 | tf_op jit(solution)/shard_map/psum | solution.py:151
Sparse Core Ops, SparseCore 0:
  65.1 107.0 all-reduce.2
  269.0 110.0 all-reduce.4
where the time goes:
time: 390 us; the launch traced here: 389 us
  waiting for transfers between devices  232 us (59%)
  local copies, waits for them, and re-layouts  61.2 us (16%)
  matrix products  29.2 us (7%)
  starting transfers between devices  26.8 us (7%)
  other arithmetic  24.3 us (6%)
  between operations  14.4 us (4%)
    psum x1, waiting for transfers between devices, broadcast(): return lax.psum(jnp.where(mine, array, jnp.zeros_like(array)), axis)  104 us
    psum x1, waiting for transfers between devices, body(): global_total = lax.psum(pool_grads[edge_base:], 'ctx')  68.8 us
    all_to_all x1, waiting for transfers between devices, body(): lax.all_to_all(outgoing_grads, 'ctx', split_axis=0, concat_axis=0, tiled=...  39.2 us
    unnamed x24, local copies, waits for them, and re-layouts  9.57 us
    all_to_all x1, waiting for transfers between devices, body(): lax.all_to_all(queries, 'head', split_axis=1, concat_axis=0, tiled=True)  8.87 us
  transfers between devices with their start and end apart: 8, of which 6 were waited for; matrix products, arithmetic and copies ran while one was open for 6% of the time, Pallas kernels for 0%

commit v1 on v0

--- a/solution.py
+++ b/solution.py
@@ -1,3 +1,4 @@
+import functools
 import math
 import jax
 import jax.numpy as jnp
@@ -11,6 +12,13 @@
 RAND = 3
 QB_DEV = 6
 NKB = 8
+
+
+def proceed_orders(here_x, axis_name):
+    return jnp.sum(lax.all_gather(here_x, axis_name=axis_name), axis=0)
+
+
+change_unit_in = functools.partial(proceed_orders, axis_name="ctx")
 
 
 def broadcast(array, axis, root):
@@ -148,7 +156,7 @@
     local_grads = local_grads + jnp.einsum(
         "dmq,dmtc->qtc", send_table, returned.astype(jnp.float32), precision=lax.Precision.HIGHEST
     )
-    global_total = lax.psum(pool_grads[edge_base:], "ctx")
+    global_total = change_unit_in(pool_grads[edge_base:])
     local_grads = local_grads.at[:G].add(
         jnp.where(myself == 0, global_total, jnp.zeros_like(global_total))
     )

time: 390 us -> 349 us (0.89)
  the two profiles are of different devices: /device:TPU:0 before, /device:TPU:13 now
where the time goes in v1:
time: 349 us; the launch traced here: 348 us
  waiting for transfers between devices  184 us (53%)
  local copies, waits for them, and re-layouts  62.4 us (18%)
  starting transfers between devices  32.2 us (9%)
  matrix products  29.2 us (8%)
  other arithmetic  26 us (7%)
  between operations  14.4 us (4%)
    psum x1, waiting for transfers between devices, broadcast(): return lax.psum(jnp.where(mine, array, jnp.zeros_like(array)), axis)  102 us
    all_to_all x1, waiting for transfers between devices, body(): lax.all_to_all(outgoing_grads, 'ctx', split_axis=0, concat_axis=0, tiled=...  65.6 us
    unnamed x24, local copies, waits for them, and re-layouts  9.57 us
    all_to_all x1, starting transfers between devices, body(): lax.all_to_all(outgoing, 'ctx', split_axis=0, concat_axis=0, tiled=True)  9.55 us
    all_to_all x1, starting transfers between devices, body(): lax.all_to_all(outgoing_grads, 'ctx', split_axis=0, concat_axis=0, tiled=...  8.4 us
    all_to_all x1, waiting for transfers between devices, body(): lax.all_to_all(queries, 'head', split_axis=1, concat_axis=0, tiled=True)  7.35 us
  transfers between devices with their start and end apart: 8, of which 5 were waited for; matrix products, arithmetic and copies ran while one was open for 9% of the time, Pallas kernels for 0%

profile of v1, /device:TPU:13, one launch (start us, length us, event | category | flops | bytes accessed | tf_op | source)
XLA Modules:
  0.0 348.1 jit_solution(5090156928285502026)
XLA Ops:
  7.2 1.8 copy.205
  9.0 3.4 all-to-all-start.2
  13.8 2.1 copy.286
  18.2 3.4 all-to-all-start.1
  21.7 3.6 %all-to-all-done.1 = bf16[384,2,128]{0,2,1:T(8,128)(2,1)S(1)} async-done(((bf16[384,2,128]{0,2,1:T(8,128)(2,1)}), bf16[384,2,128]{0,2,1:T(8,128)(2,1)S(1)}, u32[]{:S(2)}, u32[]{:S(2)}) %all-to-all-start.1) | async-done | bytes 196640 | tf_op jit(solution)/shard_map/all_to_all | solution.py:65
  25.3 3.5 %all-to-all-start = ((bf16[384,2,512]{2,0,1:T(8,128)(2,1)}), bf16[384,2,512]{2,0,1:T(8,128)(2,1)S(1)}, u32[]{:S(2)}, u32[]{:S(2)}) async-start(bf16[384,2,512]{2,0,1:T(8,128)(2,1)} %bitcast.128), calls=%async_computation | async-start | bytes 1572864 | tf_op jit(solution)/shard_map/all_to_all | solution.py:64
  30.5 7.3 %all-to-all-done = bf16[384,2,512]{2,0,1:T(8,128)(2,1)S(1)} async-done(((bf16[384,2,512]{2,0,1:T(8,128)(2,1)}), bf16[384,2,512]{2,0,1:T(8,128)(2,1)S(1)}, u32[]{:S(2)}, u32[]{:S(2)}) %all-to-all-start) | async-done | bytes 786464 | tf_op jit(solution)/shard_map/all_to_all | solution.py:64
  37.8 3.5 %all-to-all-start.4 = ((bf16[384,2,512]{2,0,1:T(8,128)(2,1)}), bf16[384,2,512]{2,0,1:T(8,128)(2,1)S(1)}, u32[]{:S(2)}, u32[]{:S(2)}) async-start(bf16[384,2,512]{2,0,1:T(8,128)(2,1)} %bitcast.127), calls=%async_computation.4 | async-start | bytes 1572864 | tf_op jit(solution)/shard_map/all_to_all | solution.py:67
  42.4 2.1 copy.215
  44.5 4.9 %all-to-all-done.4 = bf16[384,2,512]{2,0,1:T(8,128)(2,1)S(1)} async-done(((bf16[384,2,512]{2,0,1:T(8,128)(2,1)}), bf16[384,2,512]{2,0,1:T(8,128)(2,1)S(1)}, u32[]{:S(2)}, u32[]{:S(2)}) %all-to-all-start.4) | async-done | bytes 786464 | tf_op jit(solution)/shard_map/all_to_all | solution.py:67
  50.4 9.5 %all-to-all-start.3 = ((bf16[16,2,128,256]{3,2,1,0:T(8,128)(2,1)}), bf16[16,2,128,256]{3,2,1,0:T(8,128)(2,1)S(1)}, u32[]{:S(2)}, u32[]{:S(2)}) async-start(bf16[16,2,128,256]{3,2,1,0:T(8,128)(2,1)} %copy.215), calls=%async_computation.3 | async-start | bytes 4194304 | tf_op jit(solution)/shard_map/all_to_all | solution.py:110
  61.9 1.5 fusion.29
  65.6 1.7 reshape.537
  67.3 102.1 %all-reduce.2.cloned.1.call-done = bf16[2,128,256]{2,1,0:T(8,128)(2,1)} async-done(((bf16[2,128,256]{2,1,0:T(8,128)(2,1)}), bf16[2,128,256]{2,1,0:T(8,128)(2,1)}) %all-reduce.2.cloned.1.call-update) | async-done | bytes 131088 | tf_op jit(solution)/shard_map/psum | solution.py:26
  169.4 1.4 copy-done.2
  170.8 2.0 pad_maximum_fusion
  172.8 2.6 gather_fusion
  175.4 49.3 %while.13 = (s32[]{:T(128)}, bf16[6,128,4,128]{3,2,1,0:T(4,128)(2,1)}, f32[6,8,128,256]{2,3,1,0:T(8,128)}, pred[6,8]{1,0:T(8,128)(4,1)S(1)}, bf16[6,128,4,128]{3...) while((s32[]{:T(128)}, ...), condition=%wide.region_6.7_spmd, body=%wide.region_2.6_spmd.sunk | while | flops 814414336 | bytes 22569096 | solution.py:141
  175.4 1.1 dynamic-slice_bitcast_fusion.4
  224.7 3.4 convert_element_type.57
  228.1 1.1 copy-done
  229.3 3.9 %convert_select_fusion = f32[6,8,128,256]{2,3,1,0:T(8,128)} fusion(f32[6,8,128,256]{2,3,1,0:T(8,128)S(1)} %copy-done, bf16[6,8,128,256]{2,3,1,0:T(8,128)(2,1)S(1)} %convert_element_type.57, pred[6,8]{1,0:T(8,128)(4,1)S(1)} %compare_and_fusion.2), kind=kLoop, calls=%fused_computation.35 | loop fusion | flops 3145728 | bytes 15728688 | tf_op jit(solution)/shard_map/jit(_where)/select_n | solution.py:145
  233.1 6.7 %copy.226 = f32[6,8,128,256]{3,1,0,2:T(8,128)} copy(f32[6,8,128,256]{2,3,1,0:T(8,128)} %convert_select_fusion) | data formatting | bytes 12582912 | tf_op jit(solution)/shard_map/jit(_where)/select_n | solution.py:145
  239.8 5.0 %convolution_bitcast_fusion.2 = f32[40,128,256]{2,0,1:T(8,128)S(1)} fusion(f32[6,8,128,256]{3,1,0,2:T(8,128)} %copy.226, s32[6,8]{1,0:T(8,128)S(1)} %concatenate.68), kind=kOutput, calls=%fused_computation.38 | convolution fusion | flops 754976640 | bytes 11534528 | tf_op jit(solution)/shard_map/jnp,jntc->ptc/dot_general | solution.py:150
  244.9 2.3 copy-done.1
  248.0 4.5 %slice.74 = bf16[32,128,256]{2,0,1:T(8,128)(2,1)} slice(f32[40,128,256]{2,0,1:T(8,128)} %copy-done.1), slice={[6:38], [0:128], [0:256]} | slice | bytes 4194304 | tf_op jit(solution)/shard_map/slice | solution.py:153
  252.5 2.7 convert_element_type.59
  255.2 3.3 copy.227
  258.6 8.4 %all-to-all-start.5 = ((bf16[16,2,128,256]{3,1,2,0:T(2,128)(2,1)}), bf16[16,2,128,256]{3,1,2,0:T(2,128)(2,1)S(1)}, u32[]{:S(2)}, u32[]{:S(2)}) async-start(bf16[16,2,128,256]{3,1,2,0:T(2,128)(2,1)} %copy.227), calls=%async_computation.5 | async-start | bytes 4194304 | tf_op jit(solution)/shard_map/all_to_all | solution.py:155
  268.0 65.6 %all-to-all-done.5 = bf16[16,2,128,256]{3,1,2,0:T(2,128)(2,1)S(1)} async-done(((bf16[16,2,128,256]{3,1,2,0:T(2,128)(2,1)}), bf16[16,2,128,256]{3,1,2,0:T(2,128)(2,1)S(1)}, u32[]{:S(2)}, u32[]{:S(2)}) %all-to-all-start.5) | async-done | bytes 2097184 | tf_op jit(solution)/shard_map/all_to_all | solution.py:155
  333.6 3.2 fusion.24
  336.9 2.5 reduce_sum.37
  (175 shorter events, 62.8 us)
Async XLA Ops:
  7.2 8.8 %copy-start.8 = (bf16[384,256]{1,0:T(8,128)(2,1)S(1)}, bf16[384,256]{1,0:T(8,128)(2,1)}, u32[]{:S(2)}) copy-start(bf16[384,256]{1,0:T(8,128)(2,1)} %param.11) | copy-start | bytes 589828
  9.0 9.2 %all-to-all-start.2 = ((bf16[384,2,128]{0,2,1:T(8,128)(2,1)}), bf16[384,2,128]{0,2,1:T(8,128)(2,1)S(1)}, u32[]{:S(2)}, u32[]{:S(2)}) async-start(bf16[384,2,128]{0,2,1:T(8,128)(2,1)} %bitcast.24), calls=%async_computation.2 | async-start | bytes 393216 | tf_op jit(solution)/shard_map/all_to_all | solution.py:66
  13.8 15.2 %copy-start.6 = (bf16[384,1024]{1,0:T(8,128)(2,1)S(1)}, bf16[384,1024]{1,0:T(8,128)(2,1)}, u32[]{:S(2)}) copy-start(bf16[384,1024]{1,0:T(8,128)(2,1)} %param.13) | copy-start | bytes 2359300
  18.2 7.1 %all-to-all-start.1 = ((bf16[384,2,128]{0,2,1:T(8,128)(2,1)}), bf16[384,2,128]{0,2,1:T(8,128)(2,1)S(1)}, u32[]{:S(2)}, u32[]{:S(2)}) async-start(bf16[384,2,128]{0,2,1:T(8,128)(2,1)} %bitcast.21), calls=%async_computation.1 | async-start | bytes 393216 | tf_op jit(solution)/shard_map/all_to_all | solution.py:65
  25.3 12.5 %all-to-all-start = ((bf16[384,2,512]{2,0,1:T(8,128)(2,1)}), bf16[384,2,512]{2,0,1:T(8,128)(2,1)S(1)}, u32[]{:S(2)}, u32[]{:S(2)}) async-start(bf16[384,2,512]{2,0,1:T(8,128)(2,1)} %bitcast.128), calls=%async_computation | async-start | bytes 1572864 | tf_op jit(solution)/shard_map/all_to_all | solution.py:64
  30.1 12.3 %copy-start.4 = (bf16[2,384,128]{2,1,0:T(8,128)(2,1)}, bf16[2,384,128]{2,1,0:T(8,128)(2,1)S(1)}, u32[]{:S(2)}) copy-start(bf16[2,384,128]{2,1,0:T(8,128)(2,1)S(1)} %copy.206) | copy-start | bytes 589828
  30.3 7.5 %copy-start.5 = (bf16[2,384,128]{2,1,0:T(8,128)(2,1)}, bf16[2,384,128]{2,1,0:T(8,128)(2,1)S(1)}, u32[]{:S(2)}) copy-start(bf16[2,384,128]{2,1,0:T(8,128)(2,1)S(1)} %copy.204) | copy-start | bytes 589828
  37.8 11.6 %all-to-all-start.4 = ((bf16[384,2,512]{2,0,1:T(8,128)(2,1)}), bf16[384,2,512]{2,0,1:T(8,128)(2,1)S(1)}, u32[]{:S(2)}, u32[]{:S(2)}) async-start(bf16[384,2,512]{2,0,1:T(8,128)(2,1)} %bitcast.127), calls=%async_computation.4 | async-start | bytes 1572864 | tf_op jit(solution)/shard_map/all_to_all | solution.py:67
  44.5 17.0 %copy-start.9 = (s32[96]{0:T(128)S(1)}, s32[96]{0:T(128)}, u32[]{:S(2)}) copy-start(s32[96]{0:T(128)} %param.15) | copy-start | bytes 1156
  49.4 1.0 copy-start.3
  50.4 119.0 %all-to-all-start.3 = ((bf16[16,2,128,256]{3,2,1,0:T(8,128)(2,1)}), bf16[16,2,128,256]{3,2,1,0:T(8,128)(2,1)S(1)}, u32[]{:S(2)}, u32[]{:S(2)}) async-start(bf16[16,2,128,256]{3,2,1,0:T(8,128)(2,1)} %copy.215), calls=%async_computation.3 | async-start | bytes 4194304 | tf_op jit(solution)/shard_map/all_to_all | solution.py:110
  59.9 109.4 %all-reduce.2.cloned.1.call-start = ((), (), s32[]{:S(2)}) async-start(), calls=%async_computation.6 | async-start | bytes 262144 | tf_op jit(solution)/shard_map/psum | solution.py:26
  63.4 273.4 %all-gather.3.cloned.1.call-start = ((), (), s32[]{:S(2)}) async-start(), calls=%async_computation.7 | async-start | bytes 4456448 | tf_op jit(solution)/shard_map/all_gather | solution.py:18
  169.4 1.4 copy-start.2
  224.7 4.6 %copy-start = (f32[6,8,128,256]{2,3,1,0:T(8,128)S(1)}, f32[6,8,128,256]{2,3,1,0:T(8,128)}, u32[]{:S(2)}) copy-start(f32[6,8,128,256]{2,3,1,0:T(8,128)} %get-tuple-element.54) | copy-start | bytes 18874372
  244.9 2.3 copy-start.1
  258.6 8.4 %copy-start.7 = (bf16[6,128,4,128]{3,2,1,0:T(4,128)(2,1)S(1)}, bf16[6,128,4,128]{3,2,1,0:T(4,128)(2,1)}, u32[]{:S(2)}) copy-start(bf16[6,128,4,128]{3,2,1,0:T(4,128)(2,1)} %get-tuple-element.53) | copy-start | bytes 2359300
  258.6 75.0 %all-to-all-start.5 = ((bf16[16,2,128,256]{3,1,2,0:T(2,128)(2,1)}), bf16[16,2,128,256]{3,1,2,0:T(2,128)(2,1)S(1)}, u32[]{:S(2)}, u32[]{:S(2)}) async-start(bf16[16,2,128,256]{3,1,2,0:T(2,128)(2,1)} %copy.227), calls=%async_computation.5 | async-start | bytes 4194304 | tf_op jit(solution)/shard_map/all_to_all | solution.py:155
Sparse Core Ops, SparseCore 0:
  64.2 105.1 all-reduce.1
  248.1 77.2 all-gather.2
